TPU v7x, 32 devices: a whole 2x2x4 slice. The times are simulated.
32 devices in a mesh: gx: 8 (over y, x, core), gz: 4 (over z).
Axes of the slice: x: 2, y: 2, z: 4, core: 2. Of those that a mesh axis runs over, the one named last changes fastest.
Arguments:
- adjoint: float32 [5, 32, 256, 512], P(None, 'gx', None, 'gz'), may hold values from -6 to 6
- flow_state: float32 [5, 32, 256, 512], P(None, 'gx', None, 'gz'), may hold values from -6 to 6
- jacobians: float32 [3, 5, 5], replicated, may hold values from -2.5 to 2.5
- metric: float32 [3, 3, 32, 256, 512], P(None, None, 'gx', None, 'gz'), may hold values from -6 to 6
- wing_cells: int32 [32, 256, 512], P('gx', None, 'gz'), may hold values 0 or 1
- modulus: float32 [32, 256, 512], P('gz', 'gx'), may hold values from 0.5 to 2
- stiff_class: int32 [32, 256, 512], P('gz', 'gx'), may hold values from 0 to 7
- fixed_cells: int32 [32, 256, 512], P('gz', 'gx'), may hold values 0 or 1
Outputs:
- displacement: float32 [3, 32, 256, 512], P(None, 'gz', 'gx')
All inputs are finite; a program needn't handle non-finite values. No bound on the sum of `wing_cells` or of `fixed_cells` on one device may be relied on, other than what follows from the above.
Results may differ from a plain program's by a relative error of at most 0.0001.
Values sent between devices are 32-bit elements; how exact they have to be, the bound alone decides.
A program may use at most 256 MiB of HBM per device.

v0:
```python
import jax
import jax.numpy as jnp
from jax import lax
from jax.sharding import PartitionSpec as P

SWEEPS = 3


relax_factor = 0.8
mass_term = 0.5
neighbour_offsets = ((0, 1), (0, -1), (1, 1), (1, -1), (2, 1), (2, -1))


def extended_2(array, sides, width):
    for axis, dim in sides:
        devices, length = (lax.axis_size(axis), array.shape[dim])
        up = [(i, (i + 1) % devices) for i in range(devices - 1)]
        down = [(j, i) for i, j in up]
        last = lax.slice_in_dim(array, length - width, length, axis=dim)
        leading = lax.slice_in_dim(array, 0, width, axis=dim)
        before = lax.ppermute(last, axis, up)
        after = lax.ppermute(leading, axis, down)
        array = jnp.concatenate([before, array, after], axis=dim)
    return array


def offset_view(array, axis, offset):
    windows = [slice(1, array.shape[array.ndim - 3 + i] - 1) for i in range(3)]
    length = array.shape[array.ndim - 3 + axis]
    windows[axis] = slice(1 + offset, length - 1 + offset)
    leading = (slice(None),) * (array.ndim - 3)
    return array[leading + tuple(windows)]


def flow_terms(extended, jacobians, metric, wing_cells):
    adjoint_ext = extended[:5]
    state_ext = extended[5:]
    state_mid = offset_view(state_ext, 0, 0)
    wing = wing_cells.astype(jnp.float32) * state_mid[4]
    sensitivity = jnp.stack([wing * state_mid[1 + comp] for comp in range(3)])
    for direction in range(3):
        flux_ext = jnp.einsum(
            "kl,lxyz->kxyz", jacobians[direction], state_ext, precision=lax.Precision.HIGHEST
        )
        adj_lo = offset_view(adjoint_ext, direction, -1)
        adj_mid = offset_view(adjoint_ext, direction, 0)
        adj_hi = offset_view(adjoint_ext, direction, 1)
        flux_lo = offset_view(flux_ext, direction, -1)
        flux_mid = offset_view(flux_ext, direction, 0)
        flux_hi = offset_view(flux_ext, direction, 1)
        face_lower = jnp.sum((adj_mid - adj_lo) * (flux_lo + flux_mid) * 0.5, axis=0)
        face_upper = jnp.sum((adj_hi - adj_mid) * (flux_mid + flux_hi) * 0.5, axis=0)
        sensitivity = sensitivity + metric[direction] * (face_lower - face_upper)[None]
    return sensitivity


def couplings(stiff_ext):
    centre_stiff = offset_view(stiff_ext, 0, 0)
    return [
        0.5 * (centre_stiff + offset_view(stiff_ext, axis, offset))
        for axis, offset in neighbour_offsets
    ]


def diagonal_of(faces):
    total = mass_term + faces[0]
    for face in faces[1:]:
        total = total + face
    return total


def relax_sweep(field, field_ext, sensitivity, diag, free, faces):
    coupled = faces[0] * offset_view(field_ext, 0, 1)
    for index in range(1, 6):
        axis, offset = neighbour_offsets[index]
        coupled = coupled + faces[index] * offset_view(field_ext, axis, offset)
    return free * (field + relax_factor * (sensitivity - (diag * field - coupled)) / diag)


def trimmed(array, margin):
    return array[..., margin:-margin, margin:-margin, :]


def span_padded(array):
    return jnp.pad(array, [(0, 0)] * (array.ndim - 1) + [(1, 1)])


def shards(adjoint, flow_state, jacobians, metric, wing_cells, modulus, stiff_class, fixed_cells):
    stacked = jnp.concatenate([adjoint, flow_state], axis=0)
    rimmed = extended_2(stacked, (("gx", 1), ("gz", 3)), 1)
    extended = jnp.pad(rimmed, ((0, 0), (0, 0), (1, 1), (0, 0)))
    sensitivity = flow_terms(extended, jacobians, metric, wing_cells)
    mesh_source = lax.all_to_all(
        lax.all_to_all(sensitivity, "gx", split_axis=2, concat_axis=1, tiled=True),
        "gz",
        split_axis=1,
        concat_axis=3,
        tiled=True,
    )
    stiffness = modulus * jnp.exp2(-0.5 * stiff_class.astype(jnp.float32))
    signed = jnp.where(fixed_cells == 0, stiffness, -stiffness)
    signed_rim = extended_2(signed, (("gx", 1), ("gz", 0)), SWEEPS)
    stiff_all = jnp.abs(signed_rim)
    free_all = (signed_rim > 0.0).astype(jnp.float32)
    stiff_spanned = span_padded(stiff_all)
    faces = couplings(trimmed(stiff_spanned, SWEEPS - 1))
    diag = diagonal_of(faces)
    free = trimmed(free_all, SWEEPS)
    field = jnp.zeros_like(mesh_source)
    for sweep in range(SWEEPS):
        if sweep == 0:
            field_ext = jnp.zeros(
                (3, field.shape[1] + 2, field.shape[2] + 2, field.shape[3] + 2), jnp.float32
            )
        else:
            field_rim = extended_2(field, (("gx", 2), ("gz", 1)), 1)
            field_ext = span_padded(field_rim)
        field = relax_sweep(field, field_ext, mesh_source, diag, free, faces)
    return field


def solution(mesh):
    return jax.shard_map(
        shards,
        mesh=mesh,
        in_specs=(
            P(None, "gx", None, "gz"),
            P(None, "gx", None, "gz"),
            P(),
            P(None, None, "gx", None, "gz"),
            P("gx", None, "gz"),
            P("gz", "gx", None),
            P("gz", "gx", None),
            P("gz", "gx", None),
        ),
        out_specs=P(None, "gz", "gx", None),
        check_vma=False,
    )
```

profile of v0, /device:TPU:27, one launch (start us, length us, event | category | flops | bytes accessed | tf_op | source)
XLA Modules:
  0.0 298.6 jit_solution(1116262009873381882)
XLA Ops:
  0.0 5.2 %copy.53 = f32[5,4,256,128]{2,0,3,1:T(8,128)} copy(f32[5,4,256,128]{3,2,1,0:T(8,128)} %param.9) | data formatting | bytes 5242880 | tf_op args[1]
  8.6 4.3 %pad_maximum_fusion.13 = (f32[10,1,256,128]{2,0,3,1:T(8,128)S(1)}, f32[10,1,256,128]{2,0,3,1:T(8,128)}) fusion(f32[5,4,256,128]{2,0,3,1:T(8,128)} %copy.53, f32[5,4,256,128]{2,0,3,1:T(8,128)} %copy.56), kind=kLoop, calls=%fused_computation.71 | loop fusion | flops 655360 | bytes 7864320 | tf_op jit(solution)/shard_map/slice | solution.py:19
  26.1 4.7 %fusion.85 = (f32[1,3,4,256,128]{4,3,2,1,0:T(8,128)}, f32[1,3,4,256,128]{4,3,2,1,0:T(8,128)}, f32[1,3,4,256,128]{4,3,2,1,0:T(8,128)}) fusion(f32[3,3,4,256,128]{4,3,2,1,0:T(8,128)} %param.11), kind=kLoop, calls=%fused_computation.181 | loop fusion | bytes 9437184 | tf_op jit(solution)/shard_map/slice | solution.py:53
  30.8 10.9 %collective-permute-done.4 = f32[10,1,256,128]{3,2,1,0:T(8,128)} collective-permute-done((f32[10,1,256,128]{3,2,1,0:T(8,128)}, f32[10,1,256,128]{3,2,1,0:T(8,128)}, u32[]{:S(2)}, u32[]{:S(2)}) %collective-permute-start.4) | collective-permute-done | bytes 1310752 | tf_op jit(solution)/shard_map/ppermute | solution.py:21
  43.9 5.0 %collective-permute-done.5 = f32[10,1,256,128]{3,2,1,0:T(8,128)} collective-permute-done((f32[10,1,256,128]{3,2,1,0:T(8,128)}, f32[10,1,256,128]{3,2,1,0:T(8,128)}, u32[]{:S(2)}, u32[]{:S(2)}) %collective-permute-start.5) | collective-permute-done | bytes 1310752 | tf_op jit(solution)/shard_map/ppermute | solution.py:22
  54.4 4.2 %collective-permute-start.7 = (f32[10,6,256,1]{2,0,3,1:T(8,128)S(1)}, f32[10,6,256,1]{2,0,3,1:T(8,128)S(1)}, u32[]{:S(2)}, u32[]{:S(2)}) collective-permute-start(f32[10,6,256,1]{2,0,3,1:T(8,128)S(1)} %get-tuple-element.22), channel_id=1, source_target_pairs={{1,0},{2,1},{3,2},{5,4},{6,5},{7,6},{9,8},{10,9},{11,10},{13,12},{... | collective-permute-start | bytes 184328 | tf_op jit(solution)/shard_map/ppermute | solution.py:22
  60.5 16.3 %select_maximum_fusion = f32[10,6,258,130]{2,0,3,1:T(8,128)S(1)} fusion(f32[10,6,256,1]{2,0,3,1:T(8,128)S(1)} %collective-permute-done.7, f32[10,6,256,1]{2,0,3,1:T(8,128)S(1)} %collective-permute-done.6, f32[10,1,256,128]{2,0,3,1:T(8,128)S(1)} %copy-done.5, f32[10,1,256,128]{2,0,3,1:T(8,128)S(1)} %copy.55, f32[5,4,256,128]{2,0,3,1:T(8,128)S(1)} %copy-done.1, ...), kind=kLoop, calls=%fused_computation.2 | loop fusion | flops 28173600 | bytes 16036800 | tf_op jit(solution)/shard_map/concatenate | solution.py:23
  76.8 11.2 %fusion.29 = f32[5,6,258,130]{2,0,3,1:T(8,128)} fusion(f32[10,6,258,130]{2,0,3,1:T(8,128)S(1)} %select_maximum_fusion, f32[1,5,5]{2,0,1:T(1,128)S(1)} %get-tuple-element.50), kind=kOutput, calls=%fused_computation.58 | convolution fusion | flops 60372000 | bytes 13612000 | tf_op jit(solution)/shard_map/kl,lxyz->kxyz/dot_general | solution.py:42
  88.0 11.2 %fusion.32 = f32[5,6,258,130]{2,0,3,1:T(8,128)} fusion(f32[10,6,258,130]{2,0,3,1:T(8,128)S(1)} %select_maximum_fusion, f32[1,5,5]{2,0,1:T(1,128)S(1)} %get-tuple-element.49), kind=kOutput, calls=%fused_computation.59 | convolution fusion | flops 60372000 | bytes 13612000 | tf_op jit(solution)/shard_map/kl,lxyz->kxyz/dot_general | solution.py:42
  99.2 25.8 %fusion.23 = (f32[4,256,128]{1,2,0:T(8,128)}, f32[4,256,128]{1,2,0:T(8,128)}, f32[4,256,128]{1,2,0:T(8,128)S(1)}, f32[4,256,128]{1,2,0:T(8,128)S(1)}) fusion(f32[5,6,258,130]{2,0,3,1:T(8,128)} %fusion.29, f32[5,4,256,128]{2,0,3,1:T(8,128)} %copy.56, f32[10,1,256,128]{2,0,3,1:T(8,128)} %copy.59, f32[5,4,256,128]{2,0,3,1:T(8,128)} %copy.53, ...), kind=kLoop, calls=%fused_computation.47 | loop fusion | flops 15204352 | bytes 30932992 | tf_op jit(solution)/shard_map/reduce_sum | solution.py:52
  128.5 15.0 %fusion.35 = f32[5,6,258,130]{2,0,3,1:T(8,128)} fusion(f32[10,6,258,130]{2,0,3,1:T(8,128)} %copy-done, f32[1,5,5]{2,0,1:T(1,128)S(1)} %get-tuple-element.51), kind=kOutput, calls=%fused_computation.60 | convolution fusion | flops 60372000 | bytes 13609540 | tf_op jit(solution)/shard_map/kl,lxyz->kxyz/dot_general | solution.py:42
  143.5 15.2 %fusion.9 = (f32[4,256,128]{1,2,0:T(8,128)S(1)}, f32[4,256,128]{1,2,0:T(8,128)}) fusion(f32[5,6,258,130]{2,0,3,1:T(8,128)} %fusion.35, f32[5,4,256,128]{2,0,3,1:T(8,128)} %copy.56, f32[10,6,256,1]{2,0,3,1:T(8,128)S(1)} %collective-permute-done.7, f32[10,1,256,128]{2,0,3,1:T(8,128)} %copy.59, f32[10,1,256,128]{2,0,3,1:T(8,128)} %copy-done.4, ...), kind=kLoop, calls=%fused_computation.19 | loop fusion | flops 11534336 | bytes 16900096 | tf_op jit(solution)/shard_map/reduce_sum | solution.py:52
  162.1 7.7 %fusion.68 = f32[3,4,256,128]{3,1,0,2:T(4,128)S(1)} fusion(f32[1,4,256,128]{3,1,0,2:T(4,128)} %get-tuple-element.44, f32[1,4,256,128]{3,1,0,2:T(4,128)} %get-tuple-element.43, f32[1,4,256,128]{3,1,0,2:T(4,128)} %get-tuple-element.42, f32[1,3,4,256,128]{4,3,2,1,0:T(8,128)} %get-tuple-element.27, f32[1,3,4,256,128]{4,3,2,1,0:T(8,128)} %get-tuple-element.26, ...), kind=kLoop, calls=%fused_computation.122 | loop fusion | flops 3145728 | bytes 9437184 | tf_op jit(solution)/shard_map/add | solution.py:53
  169.7 22.1 %all_to_all.36 = f32[3,4,256,128]{3,1,0,2:T(4,128)S(1)} all-to-all(f32[3,4,256,128]{3,1,0,2:T(4,128)S(1)} %fusion.68), channel_id=1, replica_groups=mesh['gx'=8,'gz'=4] {'gx'}, dimensions={2} | all-to-all | bytes 3145728 | tf_op jit(solution)/shard_map/all_to_all | solution.py:94
  193.4 5.5 %all-to-all-start.1 = ((f32[3,32,32,128]{3,2,0,1:T(8,128)}), f32[3,32,32,128]{3,2,0,1:T(8,128)S(1)}, u32[]{:S(2)}, u32[]{:S(2)}) async-start(f32[3,32,32,128]{3,2,0,1:T(8,128)} %copy.76), calls=%async_computation.1 | async-start | bytes 3145728 | tf_op jit(solution)/shard_map/all_to_all | solution.py:93
  199.1 4.2 %collective-permute-start = (f32[8,3,512]{2,1,0:T(4,128)S(1)}, f32[8,3,512]{2,1,0:T(4,128)S(1)}, u32[]{:S(2)}, u32[]{:S(2)}) collective-permute-start(f32[8,3,512]{2,1,0:T(4,128)S(1)} %get-tuple-element.47), channel_id=1, source_target_pairs={{0,4},{4,8},{8,12},{12,16},{16,20},{20,24},{24,28},{1,5},{5,9},{9,... | collective-permute-start | bytes 147464 | tf_op jit(solution)/shard_map/ppermute | solution.py:21
  205.2 4.8 %collective-permute-done.1 = f32[8,3,512]{2,1,0:T(4,128)S(1)} collective-permute-done((f32[8,3,512]{2,1,0:T(4,128)S(1)}, f32[8,3,512]{2,1,0:T(4,128)S(1)}, u32[]{:S(2)}, u32[]{:S(2)}) %collective-permute-start.1) | collective-permute-done | bytes 49184 | tf_op jit(solution)/shard_map/ppermute | solution.py:22
  215.5 7.1 %collective-permute-done.2 = f32[3,38,512]{2,1,0:T(8,128)S(1)} collective-permute-done((f32[3,38,512]{2,1,0:T(8,128)S(1)}, f32[3,38,512]{2,1,0:T(8,128)S(1)}, u32[]{:S(2)}, u32[]{:S(2)}) %collective-permute-start.2) | collective-permute-done | bytes 233504 | tf_op jit(solution)/shard_map/ppermute | solution.py:21
  222.6 6.4 %collective-permute-done.3 = f32[3,38,512]{2,1,0:T(8,128)S(1)} collective-permute-done((f32[3,38,512]{2,1,0:T(8,128)S(1)}, f32[3,38,512]{2,1,0:T(8,128)S(1)}, u32[]{:S(2)}, u32[]{:S(2)}) %collective-permute-start.3) | collective-permute-done | bytes 233504 | tf_op jit(solution)/shard_map/ppermute | solution.py:22
  238.8 6.1 %collective-permute-start.8 = (f32[3,8,1,512]{3,2,1,0:T(1,128)S(1)}, f32[3,8,1,512]{3,2,1,0:T(1,128)S(1)}, u32[]{:S(2)}, u32[]{:S(2)}) collective-permute-start(f32[3,8,1,512]{3,2,1,0:T(1,128)S(1)} %get-tuple-element.38), channel_id=1, source_target_pairs={{0,4},{4,8},{8,12},{12,16},{16,20},{20,24},{24,28},{1,5},{5,9},{9,... | collective-permute-start | bytes 147464 | tf_op jit(solution)/shard_map/ppermute | solution.py:21
  247.0 4.2 %collective-permute-done.9 = f32[3,8,1,512]{3,2,1,0:T(1,128)S(1)} collective-permute-done((f32[3,8,1,512]{3,2,1,0:T(1,128)S(1)}, f32[3,8,1,512]{3,2,1,0:T(1,128)S(1)}, u32[]{:S(2)}, u32[]{:S(2)}) %collective-permute-start.9) | collective-permute-done | bytes 49184 | tf_op jit(solution)/shard_map/ppermute | solution.py:22
  251.3 8.3 %collective-permute-start.10 = (f32[3,1,34,512]{3,2,1,0:T(8,128)S(1)}, f32[3,1,34,512]{3,2,1,0:T(8,128)S(1)}, u32[]{:S(2)}, u32[]{:S(2)}) collective-permute-start(f32[3,1,34,512]{3,2,1,0:T(8,128)S(1)} %get-tuple-element.35), channel_id=1, source_target_pairs={{1,0},{2,1},{3,2},{5,4},{6,5},{7,6},{9,8},{10,9},{11,10},{13,12},{... | collective-permute-start | bytes 626696 | tf_op jit(solution)/shard_map/ppermute | solution.py:22
  264.4 4.3 %collective-permute-done.11 = f32[3,1,34,512]{3,2,1,0:T(8,128)S(1)} collective-permute-done((f32[3,1,34,512]{3,2,1,0:T(8,128)S(1)}, f32[3,1,34,512]{3,2,1,0:T(8,128)S(1)}, u32[]{:S(2)}, u32[]{:S(2)}) %collective-permute-start.11) | collective-permute-done | bytes 208928 | tf_op jit(solution)/shard_map/ppermute | solution.py:21
  277.8 4.4 %collective-permute-done.13 = f32[3,8,1,512]{3,2,1,0:T(1,128)S(1)} collective-permute-done((f32[3,8,1,512]{3,2,1,0:T(1,128)S(1)}, f32[3,8,1,512]{3,2,1,0:T(1,128)S(1)}, u32[]{:S(2)}, u32[]{:S(2)}) %collective-permute-start.13) | collective-permute-done | bytes 49184 | tf_op jit(solution)/shard_map/ppermute | solution.py:22
  (96 shorter events, 84.0 us)
Async XLA Ops:
  14.4 27.3 %collective-permute-start.4 = (f32[10,1,256,128]{3,2,1,0:T(8,128)}, f32[10,1,256,128]{3,2,1,0:T(8,128)}, u32[]{:S(2)}, u32[]{:S(2)}) collective-permute-start(f32[10,1,256,128]{3,2,1,0:T(8,128)} %copy.54), channel_id=1, source_target_pairs={{0,4},{4,8},{8,12},{12,16},{16,20},{20,24},{24,28},{1,5},{5,9},{9,... | collective-permute-start | bytes 3932168 | tf_op jit(solution)/shard_map/ppermute | solution.py:21
  21.0 27.9 %collective-permute-start.5 = (f32[10,1,256,128]{3,2,1,0:T(8,128)}, f32[10,1,256,128]{3,2,1,0:T(8,128)}, u32[]{:S(2)}, u32[]{:S(2)}) collective-permute-start(f32[10,1,256,128]{3,2,1,0:T(8,128)} %copy.57), channel_id=1, source_target_pairs={{4,0},{8,4},{12,8},{16,12},{20,16},{24,20},{28,24},{5,1},{9,5},{13... | collective-permute-start | bytes 3932168 | tf_op jit(solution)/shard_map/ppermute | solution.py:22
  43.9 55.4 %copy-start.4 = (f32[10,1,256,128]{2,0,3,1:T(8,128)}, f32[10,1,256,128]{2,0,3,1:T(8,128)S(1)}, u32[]{:S(2)}) copy-start(f32[10,1,256,128]{2,0,3,1:T(8,128)S(1)} %copy.55) | copy-start | bytes 3932164
  52.9 5.9 %collective-permute-start.6 = (f32[10,6,256,1]{2,0,3,1:T(8,128)S(1)}, f32[10,6,256,1]{2,0,3,1:T(8,128)S(1)}, u32[]{:S(2)}, u32[]{:S(2)}) collective-permute-start(f32[10,6,256,1]{2,0,3,1:T(8,128)S(1)} %get-tuple-element.21), channel_id=1, source_target_pairs={{0,1},{1,2},{2,3},{4,5},{5,6},{6,7},{8,9},{9,10},{10,11},{12,13},{... | collective-permute-start | bytes 184328 | tf_op jit(solution)/shard_map/ppermute | solution.py:21
  54.4 6.1 %collective-permute-start.7 = (f32[10,6,256,1]{2,0,3,1:T(8,128)S(1)}, f32[10,6,256,1]{2,0,3,1:T(8,128)S(1)}, u32[]{:S(2)}, u32[]{:S(2)}) collective-permute-start(f32[10,6,256,1]{2,0,3,1:T(8,128)S(1)} %get-tuple-element.22), channel_id=1, source_target_pairs={{1,0},{2,1},{3,2},{5,4},{6,5},{7,6},{9,8},{10,9},{11,10},{13,12},{... | collective-permute-start | bytes 184328 | tf_op jit(solution)/shard_map/ppermute | solution.py:22
  76.8 11.2 %copy-start = (f32[10,6,258,130]{2,0,3,1:T(8,128)}, f32[10,6,258,130]{2,0,3,1:T(8,128)S(1)}, u32[]{:S(2)}) copy-start(f32[10,6,258,130]{2,0,3,1:T(8,128)S(1)} %select_maximum_fusion) | copy-start | bytes 24148804
  128.5 15.0 %copy-start.2 = (f32[5,4,256,128]{2,0,3,1:T(8,128)S(1)}, f32[5,4,256,128]{2,0,3,1:T(8,128)}, u32[]{:S(2)}) copy-start(f32[5,4,256,128]{2,0,3,1:T(8,128)} %copy.53) | copy-start | bytes 7864324
  193.4 39.6 %all-to-all-start.1 = ((f32[3,32,32,128]{3,2,0,1:T(8,128)}), f32[3,32,32,128]{3,2,0,1:T(8,128)S(1)}, u32[]{:S(2)}, u32[]{:S(2)}) async-start(f32[3,32,32,128]{3,2,0,1:T(8,128)} %copy.76), calls=%async_computation.1 | async-start | bytes 3145728 | tf_op jit(solution)/shard_map/all_to_all | solution.py:93
  199.1 6.1 %collective-permute-start = (f32[8,3,512]{2,1,0:T(4,128)S(1)}, f32[8,3,512]{2,1,0:T(4,128)S(1)}, u32[]{:S(2)}, u32[]{:S(2)}) collective-permute-start(f32[8,3,512]{2,1,0:T(4,128)S(1)} %get-tuple-element.47), channel_id=1, source_target_pairs={{0,4},{4,8},{8,12},{12,16},{16,20},{20,24},{24,28},{1,5},{5,9},{9,... | collective-permute-start | bytes 147464 | tf_op jit(solution)/shard_map/ppermute | solution.py:21
  203.3 6.8 %collective-permute-start.1 = (f32[8,3,512]{2,1,0:T(4,128)S(1)}, f32[8,3,512]{2,1,0:T(4,128)S(1)}, u32[]{:S(2)}, u32[]{:S(2)}) collective-permute-start(f32[8,3,512]{2,1,0:T(4,128)S(1)} %get-tuple-element.48), channel_id=1, source_target_pairs={{4,0},{8,4},{12,8},{16,12},{20,16},{24,20},{28,24},{5,1},{9,5},{13... | collective-permute-start | bytes 147464 | tf_op jit(solution)/shard_map/ppermute | solution.py:22
  210.2 12.4 %collective-permute-start.2 = (f32[3,38,512]{2,1,0:T(8,128)S(1)}, f32[3,38,512]{2,1,0:T(8,128)S(1)}, u32[]{:S(2)}, u32[]{:S(2)}) collective-permute-start(f32[3,38,512]{2,1,0:T(8,128)S(1)} %get-tuple-element.45), channel_id=1, source_target_pairs={{0,1},{1,2},{2,3},{4,5},{5,6},{6,7},{8,9},{9,10},{10,11},{12,13},{... | collective-permute-start | bytes 700424 | tf_op jit(solution)/shard_map/ppermute | solution.py:21
  211.5 17.5 %collective-permute-start.3 = (f32[3,38,512]{2,1,0:T(8,128)S(1)}, f32[3,38,512]{2,1,0:T(8,128)S(1)}, u32[]{:S(2)}, u32[]{:S(2)}) collective-permute-start(f32[3,38,512]{2,1,0:T(8,128)S(1)} %get-tuple-element.46), channel_id=1, source_target_pairs={{1,0},{2,1},{3,2},{5,4},{6,5},{7,6},{9,8},{10,9},{11,10},{13,12},{... | collective-permute-start | bytes 700424 | tf_op jit(solution)/shard_map/ppermute | solution.py:22
  238.8 8.2 %collective-permute-start.8 = (f32[3,8,1,512]{3,2,1,0:T(1,128)S(1)}, f32[3,8,1,512]{3,2,1,0:T(1,128)S(1)}, u32[]{:S(2)}, u32[]{:S(2)}) collective-permute-start(f32[3,8,1,512]{3,2,1,0:T(1,128)S(1)} %get-tuple-element.38), channel_id=1, source_target_pairs={{0,4},{4,8},{8,12},{12,16},{16,20},{20,24},{24,28},{1,5},{5,9},{9,... | collective-permute-start | bytes 147464 | tf_op jit(solution)/shard_map/ppermute | solution.py:21
  244.9 6.3 %collective-permute-start.9 = (f32[3,8,1,512]{3,2,1,0:T(1,128)S(1)}, f32[3,8,1,512]{3,2,1,0:T(1,128)S(1)}, u32[]{:S(2)}, u32[]{:S(2)}) collective-permute-start(f32[3,8,1,512]{3,2,1,0:T(1,128)S(1)} %get-tuple-element.39), channel_id=1, source_target_pairs={{4,0},{8,4},{12,8},{16,12},{20,16},{24,20},{28,24},{5,1},{9,5},{13... | collective-permute-start | bytes 147464 | tf_op jit(solution)/shard_map/ppermute | solution.py:22
  251.3 13.1 %collective-permute-start.10 = (f32[3,1,34,512]{3,2,1,0:T(8,128)S(1)}, f32[3,1,34,512]{3,2,1,0:T(8,128)S(1)}, u32[]{:S(2)}, u32[]{:S(2)}) collective-permute-start(f32[3,1,34,512]{3,2,1,0:T(8,128)S(1)} %get-tuple-element.35), channel_id=1, source_target_pairs={{1,0},{2,1},{3,2},{5,4},{6,5},{7,6},{9,8},{10,9},{11,10},{13,12},{... | collective-permute-start | bytes 626696 | tf_op jit(solution)/shard_map/ppermute | solution.py:22
  259.6 10.4 %copy-start.8 = (f32[8,32,512]{2,1,0:T(8,128)S(1)}, f32[8,32,512]{2,1,0:T(8,128)}, u32[]{:S(2)}) copy-start(f32[8,32,512]{2,1,0:T(8,128)} %get-tuple-element.16) | copy-start | bytes 1572868
  259.6 10.4 %copy-start.9 = (f32[8,32,512]{2,1,0:T(8,128)S(1)}, f32[8,32,512]{2,1,0:T(8,128)}, u32[]{:S(2)}) copy-start(f32[8,32,512]{2,1,0:T(8,128)} %get-tuple-element.17) | copy-start | bytes 1572868
  259.6 10.4 %copy-start.10 = (f32[8,32,512]{2,1,0:T(8,128)S(1)}, f32[8,32,512]{2,1,0:T(8,128)}, u32[]{:S(2)}) copy-start(f32[8,32,512]{2,1,0:T(8,128)} %get-tuple-element.18) | copy-start | bytes 1572868
  259.6 10.4 %copy-start.11 = (f32[8,32,512]{2,1,0:T(8,128)S(1)}, f32[8,32,512]{2,1,0:T(8,128)}, u32[]{:S(2)}) copy-start(f32[8,32,512]{2,1,0:T(8,128)} %get-tuple-element.19) | copy-start | bytes 1572868
  259.6 9.1 %collective-permute-start.11 = (f32[3,1,34,512]{3,2,1,0:T(8,128)S(1)}, f32[3,1,34,512]{3,2,1,0:T(8,128)S(1)}, u32[]{:S(2)}, u32[]{:S(2)}) collective-permute-start(f32[3,1,34,512]{3,2,1,0:T(8,128)S(1)} %get-tuple-element.34), channel_id=1, source_target_pairs={{0,1},{1,2},{2,3},{4,5},{5,6},{6,7},{8,9},{9,10},{10,11},{12,13},{... | collective-permute-start | bytes 626696 | tf_op jit(solution)/shard_map/ppermute | solution.py:21
  272.8 5.0 %collective-permute-start.12 = (f32[3,8,1,512]{3,2,1,0:T(1,128)S(1)}, f32[3,8,1,512]{3,2,1,0:T(1,128)S(1)}, u32[]{:S(2)}, u32[]{:S(2)}) collective-permute-start(f32[3,8,1,512]{3,2,1,0:T(1,128)S(1)} %get-tuple-element.36), channel_id=1, source_target_pairs={{0,4},{4,8},{8,12},{12,16},{16,20},{20,24},{24,28},{1,5},{5,9},{9,... | collective-permute-start | bytes 147464 | tf_op jit(solution)/shard_map/ppermute | solution.py:21
  275.8 6.3 %collective-permute-start.13 = (f32[3,8,1,512]{3,2,1,0:T(1,128)S(1)}, f32[3,8,1,512]{3,2,1,0:T(1,128)S(1)}, u32[]{:S(2)}, u32[]{:S(2)}) collective-permute-start(f32[3,8,1,512]{3,2,1,0:T(1,128)S(1)} %get-tuple-element.37), channel_id=1, source_target_pairs={{4,0},{8,4},{12,8},{16,12},{20,16},{24,20},{28,24},{5,1},{9,5},{13... | collective-permute-start | bytes 147464 | tf_op jit(solution)/shard_map/ppermute | solution.py:22
  282.2 7.3 %collective-permute-start.14 = (f32[3,1,34,512]{3,2,1,0:T(8,128)S(1)}, f32[3,1,34,512]{3,2,1,0:T(8,128)S(1)}, u32[]{:S(2)}, u32[]{:S(2)}) collective-permute-start(f32[3,1,34,512]{3,2,1,0:T(8,128)S(1)} %get-tuple-element.33), channel_id=1, source_target_pairs={{1,0},{2,1},{3,2},{5,4},{6,5},{7,6},{9,8},{10,9},{11,10},{13,12},{... | collective-permute-start | bytes 626696 | tf_op jit(solution)/shard_map/ppermute | solution.py:22
  285.3 8.3 %collective-permute-start.15 = (f32[3,1,34,512]{3,2,1,0:T(8,128)S(1)}, f32[3,1,34,512]{3,2,1,0:T(8,128)S(1)}, u32[]{:S(2)}, u32[]{:S(2)}) collective-permute-start(f32[3,1,34,512]{3,2,1,0:T(8,128)S(1)} %get-tuple-element.32), channel_id=1, source_target_pairs={{0,1},{1,2},{2,3},{4,5},{5,6},{6,7},{8,9},{9,10},{10,11},{12,13},{... | collective-permute-start | bytes 626696 | tf_op jit(solution)/shard_map/ppermute | solution.py:21
  (13 other events, 82.5 us)
where the time goes:
time: 304 us; the launch traced here: 299 us
  other arithmetic  89.9 us (30%)
  waiting for transfers between devices  60.6 us (20%)
  starting transfers between devices  55.8 us (18%)
  matrix products  37.4 us (12%)
  local copies, waits for them, and re-layouts  32.2 us (11%)
  blocking collectives  22.1 us (7%)
    reduce_sum x2, other arithmetic, flow_terms(): jnp.sum((adj_hi - adj_mid) * (flux_mid + flux_hi) * 0.5, axis=0)  41 us
    dot_general x3, matrix products, flow_terms(): jnp.einsum('kl,lxyz->kxyz', jacobians[direction], state_ext, precision=la...  37.4 us
    ppermute x8, waiting for transfers between devices, extended_2(): after = lax.ppermute(leading, axis, down)  32.8 us
    ppermute x8, starting transfers between devices, extended_2(): after = lax.ppermute(leading, axis, down)  27.5 us
    ppermute x8, waiting for transfers between devices, extended_2(): before = lax.ppermute(last, axis, up)  26.5 us
    ppermute x8, starting transfers between devices, extended_2(): before = lax.ppermute(last, axis, up)  22.8 us
    all_to_all x1, blocking collectives, shards(): lax.all_to_all(sensitivity, 'gx', split_axis=2, concat_axis=1, tiled=True)  22.1 us
    concatenate x6, other arithmetic, extended_2(): array = jnp.concatenate([before, array, after], axis=dim)  19.2 us
  transfers between devices with their start and end apart: 17, of which 14 were waited for; matrix products, arithmetic and copies ran while one was open for 5% of the time, Pallas kernels for 0%

commit v1 on v0

v1 whole, which is shorter than its diff:
```python
import functools

import jax
import jax.numpy as jnp
from jax import lax
from jax.experimental import pallas as pl
from jax.experimental.pallas import tpu as pltpu
from jax.sharding import PartitionSpec as P

SWEEPS = 3
RELAX = 0.8
MASS = 0.5
PAD = 8
LANES = 128
MESH = pl.DeviceIdType.MESH
F32 = jnp.float32


def face_of(jac, d, lo_a, lo_s, hi_a, hi_s):
    both = [lo_s[l] + hi_s[l] for l in range(5)]
    total = None
    for k in range(5):
        flux = jac[d, k, 0] * both[0]
        for l in range(1, 5):
            flux = flux + jac[d, k, l] * both[l]
        term = (hi_a[k] - lo_a[k]) * flux
        total = term if total is None else total + term
    return total * 0.5


def kernel(nx, nz, jac, adj_h, st_h, met_h, wing_h, mod_h, cls_h, fix_h, out,
           adj, st, met, wing, mod, cls, fix,
           halo, zpack, zrecv, zface, fx, xface, sens, mid, recv,
           stiff, srow, srow_in, wgt, coup, field_a, field_b, frow, frow_in,
           load_sem, xh_s, xh_r, zh_s, zh_r, xf_s, xf_r,
           s1, r1, s2, r2, sp_s, sp_r, sr_s, sr_r, fp_s, fp_r, fr_s, fr_r):
    a, b = lax.axis_index("gx"), lax.axis_index("gz")
    per = nx // nz
    ny = wing.shape[1]
    half_y = ny // 2
    xt, yt, span = mod.shape
    lane = lax.broadcasted_iota(jnp.int32, (yt, LANES), 1)
    has_lo, has_hi = a > 0, a < nx - 1
    has_dn, has_up = b > 0, b < nz - 1

    loads = [
        pltpu.make_async_copy(adj_h, adj.at[:, :, pl.ds(PAD, ny), :], load_sem.at[0]),
        pltpu.make_async_copy(st_h, st.at[:, :, pl.ds(PAD, ny), :], load_sem.at[1]),
        pltpu.make_async_copy(mod_h, mod, load_sem.at[2]),
        pltpu.make_async_copy(cls_h, cls, load_sem.at[3]),
        pltpu.make_async_copy(fix_h, fix, load_sem.at[4]),
        pltpu.make_async_copy(met_h, met, load_sem.at[5]),
        pltpu.make_async_copy(wing_h, wing, load_sem.at[6]),
    ]
    for load in loads:
        load.start()

    for ref in (adj, st):
        for k in range(5):
            for x in range(4):
                ref[k, x, 0:PAD, :] = jnp.zeros((PAD, LANES), F32)
                ref[k, x, PAD + ny:, :] = jnp.zeros((PAD, LANES), F32)

    def zero(ref):
        ref[...] = jnp.zeros(ref.shape, F32)

    def zero_planes(side, z):
        stiff[z, PAD:PAD + yt, :] = jnp.zeros((yt, span), F32)
        for c in range(3):
            for f in (field_a, field_b):
                f[c, z, PAD:PAD + yt, :] = jnp.zeros((yt, span), F32)

    @pl.when(jnp.logical_not(has_lo))
    def _():
        zero(halo.at[0])
        zero(srow_in.at[0])
        zero(frow_in.at[0, 0])
        zero(frow_in.at[1, 0])

    @pl.when(jnp.logical_not(has_hi))
    def _():
        zero(halo.at[1])
        zero(srow_in.at[1])
        zero(frow_in.at[0, 1])
        zero(frow_in.at[1, 1])

    @pl.when(jnp.logical_not(has_dn))
    def _():
        zero(zrecv.at[0])
        zero_planes(0, 0)

    @pl.when(jnp.logical_not(has_up))
    def _():
        zero(zrecv.at[1])
        zero_planes(1, xt + 1)

    bar = pltpu.get_barrier_semaphore()
    for t in range(1, nx):
        pl.semaphore_signal(bar, inc=1, device_id=((a + t) % nx, b), device_id_type=MESH)
    for t in range(1, nz):
        pl.semaphore_signal(bar, inc=1, device_id=(a, (b + t) % nz), device_id_type=MESH)
    pl.semaphore_wait(bar, nx + nz - 2)

    def remote(src, dst, send, rcv, dev):
        return pltpu.make_async_remote_copy(
            src_ref=src, dst_ref=dst, send_sem=send, recv_sem=rcv,
            device_id=dev, device_id_type=MESH)

    lower, upper = (jnp.maximum(a - 1, 0), b), (jnp.minimum(a + 1, nx - 1), b)
    below, above = (a, jnp.maximum(b - 1, 0)), (a, jnp.minimum(b + 1, nz - 1))
    first, second = pl.ds(0, half_y), pl.ds(half_y, half_y)

    to_upper = [remote(src.at[:, 3, first, :], halo.at[0, i], xh_s.at[0, i], xh_r.at[0, i], upper)
                for i, src in enumerate((adj_h, st_h))]
    to_lower = [remote(src.at[:, 0, second, :], halo.at[1, i], xh_s.at[1, i], xh_r.at[1, i], lower)
                for i, src in enumerate((adj_h, st_h))]

    def start_if(cond, copies):
        @pl.when(cond)
        def _():
            for copy in copies:
                copy.start()

    def exchange_wait(cond_send, sends, cond_recv, recvs):
        @pl.when(cond_send)
        def _():
            for copy in sends:
                copy.wait_send()

        @pl.when(cond_recv)
        def _():
            for copy in recvs:
                copy.wait_recv()

    start_if(has_hi, to_upper)
    start_if(has_lo, to_lower)

    loads[0].wait()
    loads[1].wait()

    def pack_rows(n, carry):
        y0 = pl.multiple_of(n * yt, yt)
        acc = jnp.zeros((yt, LANES), F32)
        for which, ref in enumerate((adj, st)):
            for k in range(5):
                for x in range(4):
                    index = which * 20 + k * 4 + x
                    turned = pltpu.roll(ref[k, x, pl.ds(y0 + PAD, yt), :], 2 * index + 1, 1)
                    acc = jnp.where(lane // 2 == index, turned, acc)
        zpack[pl.ds(y0, yt), :] = acc
        return carry

    lax.fori_loop(0, ny // yt, pack_rows, 0)

    loads[2].wait()
    loads[3].wait()
    loads[4].wait()

    def stiff_plane(x, carry):
        value = mod[x] * jnp.exp2(-0.5 * cls[x].astype(F32))
        stiff[x + 1, PAD:PAD + yt, :] = value
        srow[0, pl.ds(x, 1), :] = value[0:1]
        srow[1, pl.ds(x, 1), :] = value[yt - 1:yt]
        return carry

    lax.fori_loop(0, xt, stiff_plane, 0)

    z_up = [remote(zpack, zrecv.at[0], zh_s.at[0], zh_r.at[0], above)]
    z_dn = [remote(zpack, zrecv.at[1], zh_s.at[1], zh_r.at[1], below)]
    start_if(has_up, z_up)
    start_if(has_dn, z_dn)
    rows = pl.ds(PAD, yt)
    sp_up = [remote(stiff.at[xt, rows, :], stiff.at[0, rows, :], sp_s.at[0], sp_r.at[0], above)]
    sp_dn = [remote(stiff.at[1, rows, :], stiff.at[xt + 1, rows, :], sp_s.at[1], sp_r.at[1], below)]
    sr_up = [remote(srow.at[1], srow_in.at[0], sr_s.at[0], sr_r.at[0], upper)]
    sr_lo = [remote(srow.at[0], srow_in.at[1], sr_s.at[1], sr_r.at[1], lower)]
    loads[5].wait()
    loads[6].wait()

    exchange_wait(has_up, z_up, has_dn, z_up)
    exchange_wait(has_dn, z_dn, has_up, z_dn)

    def zface_rows(n, carry):
        y0 = pl.multiple_of(n * yt, yt)
        mine = zpack[pl.ds(y0, yt), :]
        odd = lane % 2 == 1
        other = jnp.where(odd, pltpu.roll(zrecv[0, pl.ds(y0, yt), :], 1, 1),
                          pltpu.roll(zrecv[1, pl.ds(y0, yt), :], LANES - 1, 1))
        diff, both = mine - other, mine + other
        total = None
        states = [pltpu.roll(both, LANES - 40 - 8 * l, 1) for l in range(5)]
        for k in range(5):
            flux = jac[2, k, 0] * states[0]
            for l in range(1, 5):
                flux = flux + jac[2, k, l] * states[l]
            part = diff if k == 0 else pltpu.roll(diff, LANES - 8 * k, 1)
            total = part * flux if total is None else total + part * flux
        zface[pl.ds(y0, yt), :] = jnp.where(odd, 0.5 * total, -0.5 * total)
        return carry

    lax.fori_loop(0, ny // yt, zface_rows, 0)

    def cells(x, y0):
        ds = pl.ds(y0 + PAD, yt)
        return [adj[k, x, ds, :] for k in range(5)], [st[k, x, ds, :] for k in range(5)]

    def store_sens(half, i, x, y0, diff0):
        wide = yt + 8
        low, high = pl.ds(y0, wide), pl.ds(y0 + 1, wide)
        fy = face_of(jac, 1, [adj[k, x, low, :] for k in range(5)], [st[k, x, low, :] for k in range(5)],
                     [adj[k, x, high, :] for k in range(5)], [st[k, x, high, :] for k in range(5)])
        diff1 = fy[7:7 + yt] - fy[8:8 + yt]
        av, sv = cells(x, y0)
        fz = face_of(jac, 2, av, sv, [pltpu.roll(v, LANES - 1, 1) for v in av],
                     [pltpu.roll(v, LANES - 1, 1) for v in sv])
        edge = zface[pl.ds(y0, yt), :]
        z_hi = jnp.where(lane == LANES - 1, pltpu.roll(edge, LANES - 1 - 2 * x, 1), fz)
        z_lo = jnp.where(lane == 0, pltpu.roll(edge, LANES - 1 - 2 * x, 1), pltpu.roll(fz, 1, 1))
        diff2 = z_lo - z_hi
        ys = pl.ds(y0, yt)
        scaled = wing[x, ys, :].astype(F32) * sv[4]
        for c in range(3):
            value = scaled * sv[1 + c]
            value = value + met[0, c, x, ys, :] * diff0
            value = value + met[1, c, x, ys, :] * diff1
            value = value + met[2, c, x, ys, :] * diff2
            sens[half, i, c, ys, :] = value

    def chunk_of(t):
        return (a + 2 * nx - per * b - t) % nx

    def phase1(half, j):
        return remote(sens.at[half, :, :, pl.ds(pl.multiple_of(j * yt, yt), yt), :],
                      mid.at[half, a], s1.at[half, j], r1.at[half, a], (j, b))

    def own_chunk(half):
        return pltpu.make_async_copy(
            sens.at[half, :, :, pl.ds(pl.multiple_of(a * yt, yt), yt), :],
            mid.at[half, a], r1.at[half, a])

    def send_chunk(half, t):
        j = chunk_of(t)

        @pl.when(j != a)
        def _():
            phase1(half, j).start()

        @pl.when(j == a)
        def _():
            own_chunk(half).start()

    def slot(half, f, z):
        return recv.at[half, f % per, :, :, :, pl.ds(pl.multiple_of(z * LANES, LANES), LANES)]

    def phase2(half, f):
        return remote(mid.at[half, f], slot(half, f, b), s2.at[half, f], r2.at[half, f % per, b],
                      (a, f // per))

    def relay(half):
        def step(t, carry):
            f = (a + per * b + t) % nx
            remote(mid.at[half, f], mid.at[half, f], s1.at[half, f], r1.at[half, f], (f, b)).wait_recv()

            @pl.when(f // per != b)
            def _():
                phase2(half, f).start()

            @pl.when(f // per == b)
            def _():
                pltpu.make_async_copy(mid.at[half, f], slot(half, f, b), r2.at[half, f % per, b]).start()
            return carry

        lax.fori_loop(0, nx, step, 0)

    def make_half(half, compute):
        def step(t, carry):
            compute(pl.multiple_of(chunk_of(t) * yt, yt))

            @pl.when(t > 0)
            def _():
                send_chunk(half, t - 1)
            return carry

        lax.fori_loop(0, nx, step, 0)
        start_if(has_up, sp_up if half == 0 else [])
        start_if(has_dn, sp_dn if half == 0 else [])
        start_if(has_hi, sr_up if half == 0 else [])
        start_if(has_lo, sr_lo if half == 0 else [])
        send_chunk(half, nx - 1)

    def inner_planes(y0):
        for x in range(3):
            la, ls = cells(x, y0)
            ha, hs = cells(x + 1, y0)
            fx[x, pl.ds(y0, yt), :] = face_of(jac, 0, la, ls, ha, hs)
        for i, x in enumerate((1, 2)):
            store_sens(0, i, x, y0, fx[x - 1, pl.ds(y0, yt), :] - fx[x, pl.ds(y0, yt), :])

    make_half(0, inner_planes)
    relay(0)

    exchange_wait(has_hi, to_upper, has_lo, to_upper)
    exchange_wait(has_lo, to_lower, has_hi, to_lower)

    def bottom_rows(base):
        def step(n, carry):
            h0 = pl.multiple_of(n * yt, yt)
            ha, hs = cells(0, pl.multiple_of(h0 + base, yt))
            la = [halo[0, 0, k, pl.ds(h0, yt), :] for k in range(5)]
            ls = [halo[0, 1, k, pl.ds(h0, yt), :] for k in range(5)]
            xface[0, pl.ds(pl.multiple_of(h0 + base, yt), yt), :] = face_of(jac, 0, la, ls, ha, hs)
            return carry
        lax.fori_loop(0, half_y // yt, step, 0)

    def top_rows(base):
        def step(n, carry):
            h0 = pl.multiple_of(n * yt, yt)
            la, ls = cells(3, pl.multiple_of(h0 + base, yt))
            ha = [halo[1, 0, k, pl.ds(h0, yt), :] for k in range(5)]
            hs = [halo[1, 1, k, pl.ds(h0, yt), :] for k in range(5)]
            xface[1, pl.ds(pl.multiple_of(h0 + base, yt), yt), :] = face_of(jac, 0, la, ls, ha, hs)
            return carry
        lax.fori_loop(0, half_y // yt, step, 0)

    bottom_rows(0)
    top_rows(half_y)
    xf_lo = [remote(xface.at[0, first, :], xface.at[1, first, :], xf_s.at[0], xf_r.at[0], lower)]
    xf_up = [remote(xface.at[1, second, :], xface.at[0, second, :], xf_s.at[1], xf_r.at[1], upper)]
    start_if(has_lo, xf_lo)
    start_if(has_hi, xf_up)

    @pl.when(jnp.logical_not(has_lo))
    def _():
        bottom_rows(half_y)

    @pl.when(jnp.logical_not(has_hi))
    def _():
        top_rows(0)

    exchange_wait(has_lo, xf_lo, has_hi, xf_lo)
    exchange_wait(has_hi, xf_up, has_lo, xf_up)

    def outer_planes(y0):
        ys = pl.ds(y0, yt)
        store_sens(1, 0, 0, y0, xface[0, ys, :] - fx[0, ys, :])
        store_sens(1, 1, 3, y0, fx[2, ys, :] - xface[1, ys, :])

    make_half(1, outer_planes)

    exchange_wait(has_up, sp_up, has_dn, sp_up)
    exchange_wait(has_dn, sp_dn, has_up, sp_dn)
    exchange_wait(has_hi, sr_up, has_lo, sr_up)
    exchange_wait(has_lo, sr_lo, has_hi, sr_lo)
    relay(1)

    def put_rows(dst, src, side_row):
        dst[side_row:side_row + 1, :] = src

    def coup_plane(x, carry):
        stiff.at[x + 1][PAD - 1:PAD, :] = srow_in[0, pl.ds(x, 1), :]
        stiff.at[x + 1][PAD + yt:PAD + yt + 1, :] = srow_in[1, pl.ds(x, 1), :]
        zl = lax.broadcasted_iota(jnp.int32, (yt, span), 1)
        mid_s = stiff[x + 1, PAD:PAD + yt, :]
        around = [
            stiff[x + 2, PAD:PAD + yt, :],
            stiff[x, PAD:PAD + yt, :],
            stiff[x + 1, PAD + 1:PAD + 1 + yt, :],
            stiff[x + 1, PAD - 1:PAD - 1 + yt, :],
            jnp.where(zl == span - 1, 0.0, pltpu.roll(mid_s, span - 1, 1)),
            jnp.where(zl == 0, 0.0, pltpu.roll(mid_s, 1, 1)),
        ]
        faces = [0.5 * (mid_s + s) for s in around]
        diag = MASS + faces[0]
        for face in faces[1:]:
            diag = diag + face
        free = jnp.where(fix[x] == 0, 1.0, 0.0)
        weight = free * (RELAX / diag)
        wgt[x] = weight
        for n in range(4):
            coup[n, x] = weight * faces[n]
        coup[4, x] = jnp.where(zl == span - 1, 0.0, weight * faces[4])
        coup[5, x] = jnp.where(zl == 0, 0.0, weight * faces[5])
        return carry

    lax.fori_loop(0, xt, coup_plane, 0)

    def arrived(half):
        for h in range(per):
            for z in range(nz):
                dst = slot(half, h, z)
                remote(dst, dst, s2.at[half, 0], r2.at[half, h, z], (a, z)).wait_recv()

    arrived(0)
    arrived(1)

    def put_field(n, c, x, dst, value):
        dst[c, x + 1, PAD:PAD + yt, :] = value
        frow[n, 0, c, pl.ds(x, 1), :] = value[0:1]
        frow[n, 1, c, pl.ds(x, 1), :] = value[yt - 1:yt]

    def first_sweep(h, carry):
        for xl, (half, i) in enumerate(((1, 0), (0, 0), (0, 1), (1, 1))):
            x = h * 4 + xl
            for c in range(3):
                put_field(0, c, x, field_a, wgt[x] * recv[half, h, i, c])
        return carry

    lax.fori_loop(0, per, first_sweep, 0)

    def exchange_field(n, field):
        p_up = [remote(field.at[:, xt, rows, :], field.at[:, 0, rows, :], fp_s.at[n, 0], fp_r.at[n, 0], above)]
        p_dn = [remote(field.at[:, 1, rows, :], field.at[:, xt + 1, rows, :], fp_s.at[n, 1], fp_r.at[n, 1], below)]
        r_up = [remote(frow.at[n, 1], frow_in.at[n, 0], fr_s.at[n, 0], fr_r.at[n, 0], upper)]
        r_lo = [remote(frow.at[n, 0], frow_in.at[n, 1], fr_s.at[n, 1], fr_r.at[n, 1], lower)]
        start_if(has_up, p_up)
        start_if(has_dn, p_dn)
        start_if(has_hi, r_up)
        start_if(has_lo, r_lo)
        return p_up, p_dn, r_up, r_lo

    def relaxed(n, field, x, store):
        for c in range(3):
            field.at[c, x + 1][PAD - 1:PAD, :] = frow_in[n, 0, c, pl.ds(x, 1), :]
            field.at[c, x + 1][PAD + yt:PAD + yt + 1, :] = frow_in[n, 1, c, pl.ds(x, 1), :]
            here = field[c, x + 1, PAD:PAD + yt, :]
            total = coup[0, x] * field[c, x + 2, PAD:PAD + yt, :]
            total = total + coup[1, x] * field[c, x, PAD:PAD + yt, :]
            total = total + coup[2, x] * field[c, x + 1, PAD + 1:PAD + 1 + yt, :]
            total = total + coup[3, x] * field[c, x + 1, PAD - 1:PAD - 1 + yt, :]
            total = total + coup[4, x] * pltpu.roll(here, span - 1, 1)
            total = total + coup[5, x] * pltpu.roll(here, 1, 1)
            start = here if n == 0 else field_a[c, x + 1, PAD:PAD + yt, :]
            store(c, x, (1.0 - RELAX) * here + start + total)

    def sweep(n, field, store):
        p_up, p_dn, r_up, r_lo = exchange_field(n, field)
        exchange_wait(has_hi, r_up, has_lo, r_up)
        exchange_wait(has_lo, r_lo, has_hi, r_lo)

        def step(x, carry):
            relaxed(n, field, x, store)
            return carry

        lax.fori_loop(1, xt - 1, step, 0)
        exchange_wait(has_up, p_up, has_dn, p_up)
        exchange_wait(has_dn, p_dn, has_up, p_dn)
        relaxed(n, field, 0, store)
        relaxed(n, field, xt - 1, store)

    def store_last(c, x, value):
        out[c, x] = value

    sweep(0, field_a, lambda c, x, value: put_field(1, c, x, field_b, value))
    sweep(1, field_b, store_last)

    for half in range(2):
        def drain(t, carry, half=half):
            @pl.when(t != a)
            def _():
                phase1(half, t).wait_send()

            @pl.when(t // per != b)
            def _():
                phase2(half, t).wait_send()
            return carry

        lax.fori_loop(0, nx, drain, 0)


def shards(nx, nz, adjoint, flow_state, jacobians, metric, wing_cells, modulus, stiff_class, fixed_cells):
    ny = adjoint.shape[2]
    xt, yt, span = modulus.shape
    per = nx // nz
    V, D = pltpu.VMEM, pltpu.SemaphoreType.DMA
    anywhere = pl.BlockSpec(memory_space=pl.ANY)
    scratch = [
        V((5, 4, ny + 2 * PAD, LANES), F32),
        V((5, 4, ny + 2 * PAD, LANES), F32),
        V(metric.shape, F32),
        V(wing_cells.shape, jnp.int32),
        V(modulus.shape, F32),
        V(modulus.shape, jnp.int32),
        V(modulus.shape, jnp.int32),
        V((2, 2, 5, ny // 2, LANES), F32),
        V((ny, LANES), F32),
        V((2, ny, LANES), F32),
        V((ny, LANES), F32),
        V((3, ny, LANES), F32),
        V((2, ny, LANES), F32),
        V((2, 2, 3, ny, LANES), F32),
        V((2, nx, 2, 3, yt, LANES), F32),
        V((2, per, 2, 3, yt, span), F32),
        V((xt + 2, yt + 2 * PAD, span), F32),
        V((2, xt, span), F32),
        V((2, xt, span), F32),
        V((xt, yt, span), F32),
        V((6, xt, yt, span), F32),
        V((3, xt + 2, yt + 2 * PAD, span), F32),
        V((3, xt + 2, yt + 2 * PAD, span), F32),
        V((2, 2, 3, xt, span), F32),
        V((2, 2, 3, xt, span), F32),
        D((7,)), D((2, 2)), D((2, 2)), D((2,)), D((2,)), D((2,)), D((2,)),
        D((2, nx)), D((2, nx)), D((2, nx)), D((2, per, nz)),
        D((2,)), D((2,)), D((2,)), D((2,)),
        D((2, 2)), D((2, 2)), D((2, 2)), D((2, 2)),
    ]
    return pl.pallas_call(
        functools.partial(kernel, nx, nz),
        out_shape=jax.ShapeDtypeStruct((3, xt, yt, span), F32),
        in_specs=[pl.BlockSpec(memory_space=pltpu.SMEM)] + [anywhere] * 7,
        out_specs=pl.BlockSpec(memory_space=pltpu.VMEM),
        scratch_shapes=scratch,
        compiler_params=pltpu.CompilerParams(
            collective_id=0, has_side_effects=True, vmem_limit_bytes=63 * 1024 * 1024),
        name="adjoint_step",
    )(jacobians, adjoint, flow_state, metric, wing_cells, modulus, stiff_class, fixed_cells)


def solution(mesh):
    return jax.shard_map(
        functools.partial(shards, mesh.shape["gx"], mesh.shape["gz"]),
        mesh=mesh,
        in_specs=(
            P(None, "gx", None, "gz"),
            P(None, "gx", None, "gz"),
            P(),
            P(None, None, "gx", None, "gz"),
            P("gx", None, "gz"),
            P("gz", "gx", None),
            P("gz", "gx", None),
            P("gz", "gx", None),
        ),
        out_specs=P(None, "gz", "gx", None),
        check_vma=False,
    )
```

time: 304 us -> 79.3 us (0.26)
  the two profiles are of different devices: /device:TPU:27 before, /device:TPU:8 now
where the time goes in v1:
time: 79.3 us; the launch traced here: 79 us
  Pallas kernels  75 us (95%)
  local copies, waits for them, and re-layouts  4.05 us (5%)
    pallas_call x1, Pallas kernels, shards(): pl.pallas_call(functools.partial(kernel, nx, nz), out_shape=jax.ShapeDtyp...  75 us
    unnamed x2, local copies, waits for them, and re-layouts  4.05 us

profile of v1, /device:TPU:8, one launch (start us, length us, event | category | flops | bytes accessed | tf_op | source)
XLA Modules:
  0.0 79.0 jit_solution(3010168033908635629)
XLA Ops:
  0.0 1.3 %copy.9.jac = f32[3,5,5]{2,1,0:T(8,128)} copy(f32[3,5,5]{2,0,1:T(4,128)} %param.10) | data formatting | bytes 600 | tf_op args[2]
  1.3 75.0 %adjoint_step.1 = f32[3,8,32,512]{3,2,1,0:T(8,128)} custom-call(f32[3,5,5]{2,1,0:T(8,128)} %copy.9.jac, f32[5,4,256,128]{3,2,1,0:T(8,128)} %adj_h.1, f32[5,4,256,128]{3,2,1,0:T(8,128)} %st_h.1, f32[3,3,4,256,128]{4,3,2,1,0:T(8,128)} %met_h.1, s32[4,256,128]{2,1,0:T(8,128)} %wing_h.1, f32[8,32,512]{2,1,0:T(8,128)} %mod_h.1, s32[8,32,512]{2,1,0:T(8,128)} %cls_h.1, ...), custom_call_target="tpu_custom_call" | custom-call | tf_op jit(solution)/shard_map/adjoint_step/pallas_call | solution.py:507
  76.3 2.7 %copy.11 = f32[3,8,32,512]{3,2,1,0:T(8,128)} copy(f32[3,8,32,512]{3,2,1,0:T(8,128)} %adjoint_step.1) | data formatting | bytes 3145728

commit v2 on v1

--- a/solution.py
+++ b/solution.py
@@ -174,6 +174,19 @@
     sp_dn = [remote(stiff.at[1, rows, :], stiff.at[xt + 1, rows, :], sp_s.at[1], sp_r.at[1], below)]
     sr_up = [remote(srow.at[1], srow_in.at[0], sr_s.at[0], sr_r.at[0], upper)]
     sr_lo = [remote(srow.at[0], srow_in.at[1], sr_s.at[1], sr_r.at[1], lower)]
+    def cells(x, y0):
+        ds = pl.ds(y0 + PAD, yt)
+        return [adj[k, x, ds, :] for k in range(5)], [st[k, x, ds, :] for k in range(5)]
+
+    def inner_faces(n, carry):
+        y0 = pl.multiple_of(n * yt, yt)
+        for x in range(3):
+            la, ls = cells(x, y0)
+            ha, hs = cells(x + 1, y0)
+            fx[x, pl.ds(y0, yt), :] = face_of(jac, 0, la, ls, ha, hs)
+        return carry
+
+    lax.fori_loop(0, ny // yt, inner_faces, 0)
     loads[5].wait()
     loads[6].wait()
 
@@ -199,10 +212,6 @@
         return carry
 
     lax.fori_loop(0, ny // yt, zface_rows, 0)
-
-    def cells(x, y0):
-        ds = pl.ds(y0 + PAD, yt)
-        return [adj[k, x, ds, :] for k in range(5)], [st[k, x, ds, :] for k in range(5)]
 
     def store_sens(half, i, x, y0, diff0):
         wide = yt + 8
@@ -289,10 +298,6 @@
         send_chunk(half, nx - 1)
 
     def inner_planes(y0):
-        for x in range(3):
-            la, ls = cells(x, y0)
-            ha, hs = cells(x + 1, y0)
-            fx[x, pl.ds(y0, yt), :] = face_of(jac, 0, la, ls, ha, hs)
         for i, x in enumerate((1, 2)):
             store_sens(0, i, x, y0, fx[x - 1, pl.ds(y0, yt), :] - fx[x, pl.ds(y0, yt), :])
 
@@ -390,22 +395,22 @@
                 dst = slot(half, h, z)
                 remote(dst, dst, s2.at[half, 0], r2.at[half, h, z], (a, z)).wait_recv()
 
-    arrived(0)
-    arrived(1)
-
     def put_field(n, c, x, dst, value):
         dst[c, x + 1, PAD:PAD + yt, :] = value
         frow[n, 0, c, pl.ds(x, 1), :] = value[0:1]
         frow[n, 1, c, pl.ds(x, 1), :] = value[yt - 1:yt]
 
-    def first_sweep(h, carry):
-        for xl, (half, i) in enumerate(((1, 0), (0, 0), (0, 1), (1, 1))):
-            x = h * 4 + xl
-            for c in range(3):
-                put_field(0, c, x, field_a, wgt[x] * recv[half, h, i, c])
-        return carry
-
-    lax.fori_loop(0, per, first_sweep, 0)
+    for half, planes in enumerate(((1, 2), (0, 3))):
+        arrived(half)
+
+        def first_sweep(h, carry, half=half, planes=planes):
+            for i, xl in enumerate(planes):
+                x = h * 4 + xl
+                for c in range(3):
+                    put_field(0, c, x, field_a, wgt[x] * recv[half, h, i, c])
+            return carry
+
+        lax.fori_loop(0, per, first_sweep, 0)
 
     def exchange_field(n, field):
         p_up = [remote(field.at[:, xt, rows, :], field.at[:, 0, rows, :], fp_s.at[n, 0], fp_r.at[n, 0], above)]

time: 79.3 us -> 79.2 us (level)
  no operation moved by 1% of the time
where the time goes in v2:
time: 79.2 us; the launch traced here: 78.9 us
  Pallas kernels  74.9 us (95%)
  local copies, waits for them, and re-layouts  4.05 us (5%)
    pallas_call x1, Pallas kernels, shards(): pl.pallas_call(functools.partial(kernel, nx, nz), out_shape=jax.ShapeDtyp...  74.9 us
    unnamed x2, local copies, waits for them, and re-layouts  4.05 us

profile of v2, /device:TPU:8, one launch (start us, length us, event | category | flops | bytes accessed | tf_op | source)
XLA Modules:
  0.0 78.9 jit_solution(17123308271629920333)
XLA Ops:
  0.0 1.3 %copy.9.jac = f32[3,5,5]{2,1,0:T(8,128)} copy(f32[3,5,5]{2,0,1:T(4,128)} %param.10) | data formatting | bytes 600 | tf_op args[2]
  1.3 74.9 %adjoint_step.1 = f32[3,8,32,512]{3,2,1,0:T(8,128)} custom-call(f32[3,5,5]{2,1,0:T(8,128)} %copy.9.jac, f32[5,4,256,128]{3,2,1,0:T(8,128)} %adj_h.1, f32[5,4,256,128]{3,2,1,0:T(8,128)} %st_h.1, f32[3,3,4,256,128]{4,3,2,1,0:T(8,128)} %met_h.1, s32[4,256,128]{2,1,0:T(8,128)} %wing_h.1, f32[8,32,512]{2,1,0:T(8,128)} %mod_h.1, s32[8,32,512]{2,1,0:T(8,128)} %cls_h.1, ...), custom_call_target="tpu_custom_call" | custom-call | tf_op jit(solution)/shard_map/adjoint_step/pallas_call | solution.py:512
  76.2 2.7 %copy.11 = f32[3,8,32,512]{3,2,1,0:T(8,128)} copy(f32[3,8,32,512]{3,2,1,0:T(8,128)} %adjoint_step.1) | data formatting | bytes 3145728
